TPU v7x, 512 devices: a whole 4x4x16 slice. The times are simulated.
512 devices in a mesh: view: 32 (over y_lo, z), band: 4 (over x), batch: 4 (over y_hi, core).
Axes of the slice: x: 4, y: 4 (y_hi: 2, y_lo: 2; y = y_hi * 2 + y_lo), z: 16, core: 2. Of those that a mesh axis runs over, the one named last changes fastest.
Arguments:
- images: bfloat16 [128, 32, 16, 768], P(('batch', 'view'), 'band'), parts along dimension 0, may hold values from -6 to 6
- frame_gain: float32 [768], replicated, may hold values from 0.5 to 2.5
- frame_qkv: bfloat16 [768, 1536], replicated, may hold values from -0.3 to 0.3
- frame_out: bfloat16 [512, 768], replicated, may hold values from -0.25 to 0.25
- row1_gain: float32 [768], replicated, may hold values from 0.5 to 2.5
- row1_qkv: bfloat16 [768, 1536], P('band'), may hold values from -0.3 to 0.3
- row1_out: bfloat16 [512, 768], P(None, 'band'), may hold values from -0.25 to 0.25
- row2_gain: float32 [768], replicated, may hold values from 0.5 to 2.5
- row2_qkv: bfloat16 [768, 1536], P('band'), may hold values from -0.3 to 0.3
- row2_out: bfloat16 [512, 768], P(None, 'band'), may hold values from -0.25 to 0.25
Outputs:
- refined: bfloat16 [128, 32, 16, 768], P(('batch', 'view'), 'band'), parts along dimension 0
There are 4 independent parts, one for each index of `batch`. A program takes and returns all parts, laid end to end along the dimension named above; an argument that names none is the same for every part. Nothing has to cross between parts.
All inputs are finite; a program needn't handle non-finite values.
Results may differ from a plain program's by a relative error of at most 0.02.
Values may be sent and summed in bfloat16 or wider, within the bound.
No kernel may reach another device: no remote copies, remote signals or barrier semaphores. Data moves between devices by JAX's collectives and lax.ppermute only.
A program may use at most 64 MiB of HBM per device.

v0:
```python
import jax
import jax.numpy as jnp
from jax import lax
from jax.sharding import PartitionSpec as P

HEAD_DIM = 64
EPSILON = 1e-06
BLOCK_ROWS = 512


def rms_normed(stream, gain):
    values = stream.astype(jnp.float32)
    factor = lax.rsqrt(jnp.mean(values * values, axis=-1, keepdims=True) + EPSILON)
    return (values * factor * gain).astype(jnp.bfloat16)


def online_update(carry, queries, keys, values):
    running, total, accum = carry
    scores = jnp.einsum(
        "qhd,khd->hqk", queries, keys, preferred_element_type=jnp.float32
    ) * HEAD_DIM ** (-0.5)
    highest = jnp.maximum(running, jnp.max(scores, axis=-1))
    weights = jnp.exp(scores - highest[:, :, None])
    total = jnp.sum(weights, axis=-1)
    mixed = jnp.einsum(
        "hqk,khd->qhd", weights.astype(jnp.bfloat16), values, preferred_element_type=jnp.float32
    )
    accum = mixed
    return (highest, total, accum)


def unit_attention(trio):
    queries, keys, values = trio
    length, pair_width = queries.shape
    block = min(BLOCK_ROWS, length)
    keys = keys.reshape(length, 2, HEAD_DIM)
    values = values.reshape(length, 2, HEAD_DIM)
    blocks = queries.reshape(length // block, block, 2, HEAD_DIM)

    def one_block(query_block):
        scores = jnp.einsum(
            "qhd,khd->hqk", query_block, keys, preferred_element_type=jnp.float32
        ) * HEAD_DIM ** (-0.5)
        weights = jnp.exp(scores - jnp.max(scores, axis=-1, keepdims=True))
        mixed = jnp.einsum(
            "hqk,khd->qhd", weights.astype(jnp.bfloat16), values, preferred_element_type=jnp.float32
        )
        total = jnp.transpose(jnp.sum(weights, axis=-1))
        return (mixed / total[:, :, None]).astype(jnp.bfloat16).reshape(block, pair_width)

    return lax.map(one_block, blocks).reshape(length, pair_width)


def attend_units(pieces):
    queries, keys, values = pieces
    attended = lax.map(unit_attention, (queries[0], keys[0], values[0]))
    return lax.all_to_all(attended[None], "view", split_axis=2, concat_axis=0, tiled=True)


def project_parts(normed, shard):
    groups = shard.shape[1] // (2 * HEAD_DIM)
    piece = lax.all_gather(shard, "band", axis=0, tiled=True)
    count = piece.shape[0]
    return jnp.einsum(
        "rcd,dpw->rpcw",
        normed,
        piece.reshape(count, groups, 2 * HEAD_DIM),
        preferred_element_type=jnp.float32,
    )


def mix_parts(merged, shard):
    groups = merged.shape[1]
    piece = lax.all_gather(shard, "band", axis=1, tiled=True)
    count = piece.shape[1]
    return jnp.einsum(
        "rpcw,pwn->rcn",
        merged,
        piece.reshape(groups, 2 * HEAD_DIM, count),
        preferred_element_type=jnp.float32,
    )


def row_sublayer(stream, row_count, col_count, gain, project, mix):
    width = stream.shape[1]
    normed = rms_normed(stream, gain).reshape(row_count, col_count, width)
    projected = project(normed)
    groups = projected.shape[1] // 3
    views = lax.axis_size("view")

    def unit_layout(section):
        return section.astype(jnp.bfloat16).reshape(
            views, row_count * groups // views, col_count, 2 * HEAD_DIM
        )

    triple = (
        unit_layout(projected[:, :groups]),
        unit_layout(projected[:, groups : 2 * groups]),
        unit_layout(projected[:, 2 * groups :]),
    )
    returned = attend_units(
        (
            lax.all_to_all(triple[0], "view", split_axis=0, concat_axis=2, tiled=True),
            lax.all_to_all(triple[1], "view", split_axis=0, concat_axis=2, tiled=True),
            lax.all_to_all(triple[2], "view", split_axis=0, concat_axis=2, tiled=True),
        )
    )
    merged = returned.reshape(row_count, groups, col_count, 2 * HEAD_DIM)
    update = mix(merged).reshape(row_count * col_count, width)
    return (stream.astype(jnp.float32) + update).astype(jnp.bfloat16)


def local(
    images,
    frame_gain,
    frame_qkv,
    frame_out,
    row1_gain,
    row1_qkv,
    row1_out,
    row2_gain,
    row2_qkv,
    row2_out,
):
    _, row_count, col_count, width = images.shape
    inner = frame_out.shape[0]
    heads = inner // HEAD_DIM
    tokens = row_count * col_count
    stream = images.reshape(tokens, width)
    normed = rms_normed(stream, frame_gain)
    start_state = (
        jnp.full((heads, tokens), -1e30, jnp.float32),
        jnp.zeros((heads, tokens), jnp.float32),
        jnp.zeros((tokens, heads, HEAD_DIM), jnp.float32),
    )
    triple = jnp.dot(normed, frame_qkv, preferred_element_type=jnp.float32).astype(jnp.bfloat16)
    queries = triple[:, :inner].reshape(tokens, heads, HEAD_DIM)
    keys = lax.all_gather(triple[:, inner : 2 * inner], "band", axis=0, tiled=True)
    values = lax.all_gather(triple[:, 2 * inner :], "band", axis=0, tiled=True)
    count = keys.shape[0]
    result = online_update(
        start_state,
        queries,
        keys.reshape(count, heads, HEAD_DIM),
        values.reshape(count, heads, HEAD_DIM),
    )
    _, total, accum = result
    attended = (
        (accum / jnp.transpose(total)[:, :, None]).astype(jnp.bfloat16).reshape(tokens, inner)
    )
    update = jnp.dot(attended, frame_out, preferred_element_type=jnp.float32)
    stream = (stream.astype(jnp.float32) + update).astype(jnp.bfloat16)
    stream = row_sublayer(
        stream,
        row_count,
        col_count,
        row1_gain,
        lambda normed_rows: project_parts(normed_rows, row1_qkv),
        lambda merged: mix_parts(merged, row1_out),
    )
    stream = row_sublayer(
        stream,
        row_count,
        col_count,
        row2_gain,
        lambda normed_rows: project_parts(normed_rows, row2_qkv),
        lambda merged: mix_parts(merged, row2_out),
    )
    return stream.reshape(images.shape)


def solution(mesh):
    in_specs = (
        P(("batch", "view"), "band", None, None),
        P(),
        P(),
        P(),
        P(),
        P("band", None),
        P(None, "band"),
        P(),
        P("band", None),
        P(None, "band"),
    )
    out_specs = P(("batch", "view"), "band", None, None)
    return jax.shard_map(local, mesh=mesh, in_specs=in_specs, out_specs=out_specs, check_vma=False)
```

profile of v0, /device:TPU:8, one launch (start us, length us, event | category | flops | bytes accessed | tf_op | source)
XLA Modules:
  0.0 268.4 jit_solution(17750390809118338394)
XLA Ops:
  11.4 13.1 %all_gather.19 = bf16[512,512]{1,0:T(8,128)(2,1)S(1)} all-gather(bf16[128,512]{1,0:T(8,128)(2,1)S(1)} %get-tuple-element.74), channel_id=1, replica_groups=mesh['view'=32,'band'=4,'batch'=4] {'band'}, dimensions={0}, use_global_device_ids=true | all-gather | bytes 655360 | tf_op jit(solution)/shard_map/all_gather | solution.py:138
  25.8 1.9 multiply_reduce_fusion.2
  27.6 15.3 %all_gather.18 = bf16[512,512]{1,0:T(8,128)(2,1)S(1)} all-gather(bf16[128,512]{1,0:T(8,128)(2,1)S(1)} %get-tuple-element.82), channel_id=1, replica_groups=mesh['view'=32,'band'=4,'batch'=4] {'band'}, dimensions={0}, use_global_device_ids=true | all-gather | bytes 655360 | tf_op jit(solution)/shard_map/all_gather | solution.py:139
  43.2 2.3 fusion
  47.2 9.3 %all-gather.3.cloned.1.call-done = bf16[768,1536]{1,0:T(8,128)(2,1)} async-done(((bf16[192,1536]{1,0:T(8,128)(2,1)}), bf16[768,1536]{1,0:T(8,128)(2,1)}) %all-gather.3.cloned.1.call-update) | async-done | bytes 2359312 | tf_op jit(solution)/shard_map/all_gather | solution.py:62
  56.6 4.3 %copy.50 = bf16[768,1536]{0,1:T(8,128)(2,1)} copy(bf16[768,1536]{1,0:T(8,128)(2,1)} %all-gather.3.cloned.1.call-done) | data formatting | bytes 4718592 | tf_op jit(solution)/shard_map/all_gather | solution.py:62
  60.8 2.6 fusion.6
  64.1 30.6 %all_to_all.32 = bf16[32,1,16,128]{3,2,1,0:T(8,128)(2,1)S(1)} all-to-all(bf16[32,1,16,128]{3,2,1,0:T(8,128)(2,1)S(1)} %bitcast.147), channel_id=1, replica_groups=mesh['view'=32,'band'=4,'batch'=4] {'view'}, dimensions={0} | all-to-all | bytes 262144 | tf_op jit(solution)/shard_map/all_to_all | solution.py:104
  94.7 19.1 %all_to_all.33 = bf16[32,1,16,128]{3,2,1,0:T(8,128)(2,1)S(1)} all-to-all(bf16[32,1,16,128]{3,2,1,0:T(8,128)(2,1)S(1)} %bitcast.145), channel_id=1, replica_groups=mesh['view'=32,'band'=4,'batch'=4] {'view'}, dimensions={0} | all-to-all | bytes 262144 | tf_op jit(solution)/shard_map/all_to_all | solution.py:103
  113.8 5.1 %all-to-all-start = ((bf16[32,1,16,128]{3,2,1,0:T(8,128)(2,1)}), bf16[32,1,16,128]{3,2,1,0:T(8,128)(2,1)S(1)}, u32[]{:S(2)}, u32[]{:S(2)}) async-start(bf16[32,1,16,128]{3,2,1,0:T(8,128)(2,1)} %bitcast.14), calls=%async_computation | async-start | bytes 262144 | tf_op jit(solution)/shard_map/all_to_all | solution.py:105
  119.2 13.9 %all-to-all-done = bf16[32,1,16,128]{3,2,1,0:T(8,128)(2,1)S(1)} async-done(((bf16[32,1,16,128]{3,2,1,0:T(8,128)(2,1)}), bf16[32,1,16,128]{3,2,1,0:T(8,128)(2,1)S(1)}, u32[]{:S(2)}, u32[]{:S(2)}) %all-to-all-start) | async-done | bytes 131104 | tf_op jit(solution)/shard_map/all_to_all | solution.py:105
  138.3 5.9 %all-to-all-start.3 = ((bf16[32,2,1024]{2,1,0:T(2,128)(2,1)}), bf16[32,2,1024]{2,1,0:T(2,128)(2,1)}, u32[]{:S(2)}, u32[]{:S(2)}) async-start(bf16[32,2,1024]{2,1,0:T(2,128)(2,1)} %reshape.216), calls=%async_computation.3 | async-start | bytes 262144 | tf_op jit(solution)/shard_map/all_to_all | solution.py:57
  144.2 13.5 %all_gather.21 = bf16[512,768]{0,1:T(8,128)(2,1)S(1)} all-gather(bf16[512,192]{0,1:T(8,128)(2,1)} %param.16), channel_id=1, replica_groups=mesh['view'=32,'band'=4,'batch'=4] {'band'}, dimensions={1}, use_global_device_ids=true | all-gather | bytes 983040 | tf_op jit(solution)/shard_map/all_gather | solution.py:74
  158.9 4.3 %copy.62 = bf16[768,1536]{0,1:T(8,128)(2,1)} copy(bf16[768,1536]{1,0:T(8,128)(2,1)} %all-gather.5.cloned.1.call-done) | data formatting | bytes 4718592 | tf_op jit(solution)/shard_map/all_gather | solution.py:62
  164.6 1.6 multiply_reduce_fusion.3
  168.1 27.2 %all_to_all.34 = bf16[32,1,16,128]{3,2,1,0:T(8,128)(2,1)S(1)} all-to-all(bf16[32,1,16,128]{3,2,1,0:T(8,128)(2,1)S(1)} %bitcast.148), channel_id=1, replica_groups=mesh['view'=32,'band'=4,'batch'=4] {'view'}, dimensions={0} | all-to-all | bytes 262144 | tf_op jit(solution)/shard_map/all_to_all | solution.py:104
  195.3 18.5 %all_to_all.35 = bf16[32,1,16,128]{3,2,1,0:T(8,128)(2,1)S(1)} all-to-all(bf16[32,1,16,128]{3,2,1,0:T(8,128)(2,1)S(1)} %bitcast.146), channel_id=1, replica_groups=mesh['view'=32,'band'=4,'batch'=4] {'view'}, dimensions={0} | all-to-all | bytes 262144 | tf_op jit(solution)/shard_map/all_to_all | solution.py:103
  213.8 5.2 %all-to-all-start.4 = ((bf16[32,1,16,128]{3,2,1,0:T(8,128)(2,1)}), bf16[32,1,16,128]{3,2,1,0:T(8,128)(2,1)S(1)}, u32[]{:S(2)}, u32[]{:S(2)}) async-start(bf16[32,1,16,128]{3,2,1,0:T(8,128)(2,1)} %bitcast.33), calls=%async_computation.4 | async-start | bytes 262144 | tf_op jit(solution)/shard_map/all_to_all | solution.py:105
  221.4 11.8 %all-to-all-done.4 = bf16[32,1,16,128]{3,2,1,0:T(8,128)(2,1)S(1)} async-done(((bf16[32,1,16,128]{3,2,1,0:T(8,128)(2,1)}), bf16[32,1,16,128]{3,2,1,0:T(8,128)(2,1)S(1)}, u32[]{:S(2)}, u32[]{:S(2)}) %all-to-all-start.4) | async-done | bytes 131104 | tf_op jit(solution)/shard_map/all_to_all | solution.py:105
  233.4 2.1 fusion.19
  237.8 5.1 %all-to-all-start.7 = ((bf16[32,2,1024]{2,1,0:T(2,128)(2,1)}), bf16[32,2,1024]{2,1,0:T(2,128)(2,1)S(1)}, u32[]{:S(2)}, u32[]{:S(2)}) async-start(bf16[32,2,1024]{2,1,0:T(2,128)(2,1)} %reshape.218), calls=%async_computation.7 | async-start | bytes 262144 | tf_op jit(solution)/shard_map/all_to_all | solution.py:57
  243.0 14.1 %all_gather.23 = bf16[512,768]{0,1:T(8,128)(2,1)} all-gather(bf16[512,192]{0,1:T(8,128)(2,1)S(1)} %copy-done.7), channel_id=1, replica_groups=mesh['view'=32,'band'=4,'batch'=4] {'band'}, dimensions={1}, use_global_device_ids=true | all-gather | bytes 983040 | tf_op jit(solution)/shard_map/all_gather | solution.py:74
  257.0 2.3 copy.73
  259.5 2.1 fusion.10
  (71 shorter events, 23.4 us)
Async XLA Ops:
  6.5 3.7 %copy-start = (bf16[768,1536]{1,0:T(8,128)(2,1)S(1)}, bf16[768,1536]{1,0:T(8,128)(2,1)}, u32[]{:S(2)}) copy-start(bf16[768,1536]{1,0:T(8,128)(2,1)} %param.12) | copy-start | bytes 7077892
  6.5 50.0 %all-gather.3.cloned.1.call-start = ((), (), s32[]{:S(2)}) async-start(), calls=%async_computation.8 | async-start | bytes 2949120 | tf_op jit(solution)/shard_map/all_gather | solution.py:62
  7.3 151.7 %all-gather.5.cloned.1.call-start = ((), (), s32[]{:S(2)}) async-start(), calls=%async_computation.9 | async-start | bytes 2949120 | tf_op jit(solution)/shard_map/all_gather | solution.py:62
  43.2 2.3 copy-start.3
  45.5 0.9 copy-start.4
  45.5 1.2 copy-start.5
  45.5 1.6 copy-start.8
  113.8 19.3 %all-to-all-start = ((bf16[32,1,16,128]{3,2,1,0:T(8,128)(2,1)}), bf16[32,1,16,128]{3,2,1,0:T(8,128)(2,1)S(1)}, u32[]{:S(2)}, u32[]{:S(2)}) async-start(bf16[32,1,16,128]{3,2,1,0:T(8,128)(2,1)} %bitcast.14), calls=%async_computation | async-start | bytes 262144 | tf_op jit(solution)/shard_map/all_to_all | solution.py:105
  134.0 0.9 copy-start.6
  138.3 24.9 %all-to-all-start.3 = ((bf16[32,2,1024]{2,1,0:T(2,128)(2,1)}), bf16[32,2,1024]{2,1,0:T(2,128)(2,1)}, u32[]{:S(2)}, u32[]{:S(2)}) async-start(bf16[32,2,1024]{2,1,0:T(2,128)(2,1)} %reshape.216), calls=%async_computation.3 | async-start | bytes 262144 | tf_op jit(solution)/shard_map/all_to_all | solution.py:57
  163.2 3.1 %copy-start.9 = (f32[768]{0:T(1024)S(1)}, f32[768]{0:T(1024)}, u32[]{:S(2)}) copy-start(f32[768]{0:T(1024)} %param.17) | copy-start | bytes 9220
  164.6 1.9 copy-start.1
  213.8 19.5 %all-to-all-start.4 = ((bf16[32,1,16,128]{3,2,1,0:T(8,128)(2,1)}), bf16[32,1,16,128]{3,2,1,0:T(8,128)(2,1)S(1)}, u32[]{:S(2)}, u32[]{:S(2)}) async-start(bf16[32,1,16,128]{3,2,1,0:T(8,128)(2,1)} %bitcast.33), calls=%async_computation.4 | async-start | bytes 262144 | tf_op jit(solution)/shard_map/all_to_all | solution.py:105
  219.7 1.4 copy-start.2
  233.4 9.6 %copy-start.7 = (bf16[512,192]{0,1:T(8,128)(2,1)S(1)}, bf16[512,192]{0,1:T(8,128)(2,1)}, u32[]{:S(2)}) copy-start(bf16[512,192]{0,1:T(8,128)(2,1)} %param.19) | copy-start | bytes 589828
  237.8 21.5 %all-to-all-start.7 = ((bf16[32,2,1024]{2,1,0:T(2,128)(2,1)}), bf16[32,2,1024]{2,1,0:T(2,128)(2,1)S(1)}, u32[]{:S(2)}, u32[]{:S(2)}) async-start(bf16[32,2,1024]{2,1,0:T(2,128)(2,1)} %reshape.218), calls=%async_computation.7 | async-start | bytes 262144 | tf_op jit(solution)/shard_map/all_to_all | solution.py:57
Sparse Core Ops, SparseCore 0:
  9.4 47.0 all-gather.2
  58.6 41.9 all-gather.4
where the time goes:
time: 269 us; the launch traced here: 268 us
  blocking collectives  152 us (57%)
  waiting for transfers between devices  36.4 us (14%)
  local copies, waits for them, and re-layouts  23.1 us (9%)
  starting transfers between devices  21.3 us (8%)
  matrix products  14 us (5%)
  between operations  13.8 us (5%)
  other arithmetic  8.23 us (3%)
    all_to_all x2, blocking collectives, row_sublayer(): lax.all_to_all(triple[1], 'view', split_axis=0, concat_axis=2, tiled=True)  57.8 us
    all_to_all x2, blocking collectives, row_sublayer(): lax.all_to_all(triple[0], 'view', split_axis=0, concat_axis=2, tiled=True)  37.7 us
    all_gather x2, blocking collectives, mix_parts(): piece = lax.all_gather(shard, 'band', axis=1, tiled=True)  27.6 us
    all_to_all x2, waiting for transfers between devices, row_sublayer(): lax.all_to_all(triple[2], 'view', split_axis=0, concat_axis=2, tiled=True)  25.7 us
    all_gather x1, blocking collectives, local(): values = lax.all_gather(triple[:, 2 * inner:], 'band', axis=0, tiled=True)  15.3 us
    all_gather x1, blocking collectives, local(): lax.all_gather(triple[:, inner:2 * inner], 'band', axis=0, tiled=True)  13.1 us
    all_to_all x2, starting transfers between devices, attend_units(): lax.all_to_all(attended[None], 'view', split_axis=2, concat_axis=0, tiled...  11 us
    all_to_all x2, starting transfers between devices, row_sublayer(): lax.all_to_all(triple[2], 'view', split_axis=0, concat_axis=2, tiled=True)  10.3 us
  transfers between devices with their start and end apart: 6, of which 3 were waited for; matrix products, arithmetic and copies ran while one was open for 12% of the time, Pallas kernels for 0%

commit v1 on v0

--- a/solution.py
+++ b/solution.py
@@ -59,7 +59,16 @@
 
 def project_parts(normed, shard):
     groups = shard.shape[1] // (2 * HEAD_DIM)
-    piece = lax.all_gather(shard, "band", axis=0, tiled=True)
+    _fit_loads = lambda mine, net_axis: jnp.concatenate(
+        lax.all_to_all(
+            jnp.stack([mine for _ in range(lax.axis_size(net_axis))], 0),
+            concat_axis=0,
+            split_axis=0,
+            axis_name=net_axis,
+        ),
+        0,
+    )
+    piece = _fit_loads(shard, "band")
     count = piece.shape[0]
     return jnp.einsum(
         "rcd,dpw->rpcw",

time: 269 us -> 298 us (1.11)
  blocking collectives: 152 us -> 195 us
  between operations: 13.8 us -> 0.38 us
  waiting for transfers between devices: 36.4 us -> 27.5 us
  local copies, waits for them, and re-layouts: 23.1 us -> 29 us
  starting transfers between devices: 21.3 us -> 25.6 us
  other arithmetic: 8.23 us -> 4.39 us
    all_gather x1, blocking collectives: 13.1 us -> 36.8 us  [local(): lax.all_gather(triple[:, inner:2 * inner], 'band', axis=0, tiled=True)]
    all_to_all x0 -> x1, blocking collectives: none -> 18.4 us  [row_sublayer(): lax.all_to_all(triple[2], 'view', split_axis=0, concat_axis=2, tiled=True)]
    all_to_all x0 -> x2, waiting for transfers between devices: none -> 15.6 us  [project_parts(): lax.all_to_all(jnp.stack([mine for _ in range(lax.axis_size(net_axis))],...]
    another operation x0 -> x4, local copies, waits for them, and re-layouts: none -> 15.3 us  [the longest x2 10.9 us: project_parts(): piece.reshape(count, groups, 2 * HEAD_DIM)]
    all_to_all x2 -> x1, waiting for transfers between devices: 25.7 us -> 11.8 us  [row_sublayer(): lax.all_to_all(triple[2], 'view', split_axis=0, concat_axis=2, tiled=True)]
    all_gather x2 -> x0, waiting for transfers between devices: 9.32 us -> none  [project_parts(): piece = lax.all_gather(shard, 'band', axis=0, tiled=True)]
    all_to_all x0 -> x2, starting transfers between devices: none -> 9.11 us  [project_parts(): lax.all_to_all(jnp.stack([mine for _ in range(lax.axis_size(net_axis))],...]
    all_gather x2 -> x0, local copies, waits for them, and re-layouts: 8.55 us -> none  [project_parts(): piece = lax.all_gather(shard, 'band', axis=0, tiled=True)]
  transfers between devices with their start and end apart: 6 -> 5, of which waited for: 3 -> 2; matrix products, arithmetic and copies ran while one was open for 12% -> 7% of each run, Pallas kernels for 0% -> 0%
where the time goes in v1:
time: 298 us; the launch traced here: 297 us
  blocking collectives  195 us (65%)
  local copies, waits for them, and re-layouts  29 us (10%)
  waiting for transfers between devices  27.5 us (9%)
  starting transfers between devices  25.6 us (9%)
  matrix products  15.1 us (5%)
  other arithmetic  4.39 us (1%)
    all_to_all x2, blocking collectives, row_sublayer(): lax.all_to_all(triple[1], 'view', split_axis=0, concat_axis=2, tiled=True)  59 us
    all_to_all x2, blocking collectives, row_sublayer(): lax.all_to_all(triple[0], 'view', split_axis=0, concat_axis=2, tiled=True)  39.6 us
    all_gather x1, blocking collectives, local(): lax.all_gather(triple[:, inner:2 * inner], 'band', axis=0, tiled=True)  36.8 us
    all_gather x2, blocking collectives, mix_parts(): piece = lax.all_gather(shard, 'band', axis=1, tiled=True)  27.6 us
    all_to_all x1, blocking collectives, row_sublayer(): lax.all_to_all(triple[2], 'view', split_axis=0, concat_axis=2, tiled=True)  18.4 us
    all_to_all x2, waiting for transfers between devices, project_parts(): lax.all_to_all(jnp.stack([mine for _ in range(lax.axis_size(net_axis))],...  15.6 us
    all_gather x1, blocking collectives, local(): values = lax.all_gather(triple[:, 2 * inner:], 'band', axis=0, tiled=True)  13.4 us
    all_to_all x1, waiting for transfers between devices, row_sublayer(): lax.all_to_all(triple[2], 'view', split_axis=0, concat_axis=2, tiled=True)  11.8 us
  transfers between devices with their start and end apart: 5, of which 2 were waited for; matrix products, arithmetic and copies ran while one was open for 7% of the time, Pallas kernels for 0%

profile of v1, /device:TPU:8, one launch (start us, length us, event | category | flops | bytes accessed | tf_op | source)
XLA Modules:
  0.0 296.7 jit_solution(15867715329649235236)
XLA Ops:
  0.0 2.8 stack.4
  2.8 4.6 %all-to-all-start = ((bf16[4,192,1536]{2,1,0:T(8,128)(2,1)}), bf16[4,192,1536]{2,1,0:T(8,128)(2,1)}, u32[]{:S(2)}, u32[]{:S(2)}) async-start(bf16[4,192,1536]{2,1,0:T(8,128)(2,1)} %stack.4), calls=%async_computation | async-start | bytes 4718592 | tf_op jit(solution)/shard_map/all_to_all | solution.py:63
  8.3 36.8 %all_gather.13 = bf16[512,512]{1,0:T(8,128)(2,1)S(1)} all-gather(bf16[128,512]{1,0:T(8,128)(2,1)S(1)} %get-tuple-element.74), channel_id=1, replica_groups=mesh['view'=32,'band'=4,'batch'=4] {'band'}, dimensions={0}, use_global_device_ids=true | all-gather | bytes 655360 | tf_op jit(solution)/shard_map/all_gather | solution.py:147
  45.1 13.4 %all_gather.12 = bf16[512,512]{1,0:T(8,128)(2,1)S(1)} all-gather(bf16[128,512]{1,0:T(8,128)(2,1)S(1)} %get-tuple-element.82), channel_id=1, replica_groups=mesh['view'=32,'band'=4,'batch'=4] {'band'}, dimensions={0}, use_global_device_ids=true | all-gather | bytes 655360 | tf_op jit(solution)/shard_map/all_gather | solution.py:148
  64.5 5.4 %reshape_reshape.6 = bf16[768,12,128]{2,1,0:T(8,128)(2,1)} reshape(bf16[4,192,1536]{2,1,0:T(8,128)(2,1)} %all-to-all-done) | data formatting | bytes 4718592 | tf_op jit(solution)/shard_map/reshape;reshape | solution.py:76
  70.0 2.5 fusion.21
  72.5 30.9 %all_to_all.40 = bf16[32,1,16,128]{3,2,1,0:T(8,128)(2,1)S(1)} all-to-all(bf16[32,1,16,128]{3,2,1,0:T(8,128)(2,1)S(1)} %bitcast.150), channel_id=1, replica_groups=mesh['view'=32,'band'=4,'batch'=4] {'view'}, dimensions={0} | all-to-all | bytes 262144 | tf_op jit(solution)/shard_map/all_to_all | solution.py:113
  103.4 18.5 %all_to_all.41 = bf16[32,1,16,128]{3,2,1,0:T(8,128)(2,1)S(1)} all-to-all(bf16[32,1,16,128]{3,2,1,0:T(8,128)(2,1)S(1)} %bitcast.148), channel_id=1, replica_groups=mesh['view'=32,'band'=4,'batch'=4] {'view'}, dimensions={0} | all-to-all | bytes 262144 | tf_op jit(solution)/shard_map/all_to_all | solution.py:112
  121.9 18.4 %all_to_all.84 = bf16[32,1,16,128]{3,2,1,0:T(8,128)(2,1)S(1)} all-to-all(bf16[32,1,16,128]{3,2,1,0:T(8,128)(2,1)S(1)} %bitcast.147), channel_id=1, replica_groups=mesh['view'=32,'band'=4,'batch'=4] {'view'}, dimensions={0} | all-to-all | bytes 262144 | tf_op jit(solution)/shard_map/all_to_all | solution.py:114
  141.9 4.5 %all-to-all-start.5 = ((bf16[4,192,1536]{2,1,0:T(8,128)(2,1)}), bf16[4,192,1536]{2,1,0:T(8,128)(2,1)}, u32[]{:S(2)}, u32[]{:S(2)}) async-start(bf16[4,192,1536]{2,1,0:T(8,128)(2,1)} %stack.5), calls=%async_computation.5 | async-start | bytes 4718592 | tf_op jit(solution)/shard_map/all_to_all | solution.py:63
  151.6 15.6 %all-to-all-done.5 = bf16[4,192,1536]{2,1,0:T(8,128)(2,1)} async-done(((bf16[4,192,1536]{2,1,0:T(8,128)(2,1)}), bf16[4,192,1536]{2,1,0:T(8,128)(2,1)}, u32[]{:S(2)}, u32[]{:S(2)}) %all-to-all-start.5) | async-done | bytes 2359328 | tf_op jit(solution)/shard_map/all_to_all | solution.py:63
  167.2 5.6 %all-to-all-start.4 = ((bf16[32,2,1024]{2,1,0:T(2,128)(2,1)}), bf16[32,2,1024]{2,1,0:T(2,128)(2,1)}, u32[]{:S(2)}, u32[]{:S(2)}) async-start(bf16[32,2,1024]{2,1,0:T(2,128)(2,1)} %reshape.212), calls=%async_computation.4 | async-start | bytes 262144 | tf_op jit(solution)/shard_map/all_to_all | solution.py:57
  172.9 13.5 %all_gather.14 = bf16[512,768]{0,1:T(8,128)(2,1)S(1)} all-gather(bf16[512,192]{0,1:T(8,128)(2,1)} %param.16), channel_id=1, replica_groups=mesh['view'=32,'band'=4,'batch'=4] {'band'}, dimensions={1}, use_global_device_ids=true | all-gather | bytes 983040 | tf_op jit(solution)/shard_map/all_gather | solution.py:83
  187.6 5.4 %reshape_reshape.7 = bf16[768,12,128]{2,1,0:T(8,128)(2,1)} reshape(bf16[4,192,1536]{2,1,0:T(8,128)(2,1)} %all-to-all-done.5) | data formatting | bytes 4718592 | tf_op jit(solution)/shard_map/reshape;reshape | solution.py:76
  196.1 2.4 fusion.18
  199.2 28.1 %all_to_all.85 = bf16[32,1,16,128]{3,2,1,0:T(8,128)(2,1)S(1)} all-to-all(bf16[32,1,16,128]{3,2,1,0:T(8,128)(2,1)S(1)} %bitcast.151), channel_id=1, replica_groups=mesh['view'=32,'band'=4,'batch'=4] {'view'}, dimensions={0} | all-to-all | bytes 262144 | tf_op jit(solution)/shard_map/all_to_all | solution.py:113
  227.4 21.1 %all_to_all.86 = bf16[32,1,16,128]{3,2,1,0:T(8,128)(2,1)S(1)} all-to-all(bf16[32,1,16,128]{3,2,1,0:T(8,128)(2,1)S(1)} %bitcast.149), channel_id=1, replica_groups=mesh['view'=32,'band'=4,'batch'=4] {'view'}, dimensions={0} | all-to-all | bytes 262144 | tf_op jit(solution)/shard_map/all_to_all | solution.py:112
  248.5 5.7 %all-to-all-start.6 = ((bf16[32,1,16,128]{3,2,1,0:T(8,128)(2,1)}), bf16[32,1,16,128]{3,2,1,0:T(8,128)(2,1)S(1)}, u32[]{:S(2)}, u32[]{:S(2)}) async-start(bf16[32,1,16,128]{3,2,1,0:T(8,128)(2,1)} %bitcast.31), calls=%async_computation.6 | async-start | bytes 262144 | tf_op jit(solution)/shard_map/all_to_all | solution.py:114
  256.6 11.8 %all-to-all-done.6 = bf16[32,1,16,128]{3,2,1,0:T(8,128)(2,1)S(1)} async-done(((bf16[32,1,16,128]{3,2,1,0:T(8,128)(2,1)}), bf16[32,1,16,128]{3,2,1,0:T(8,128)(2,1)S(1)}, u32[]{:S(2)}, u32[]{:S(2)}) %all-to-all-start.6) | async-done | bytes 131104 | tf_op jit(solution)/shard_map/all_to_all | solution.py:114
  268.6 2.1 fusion.35
  272.9 5.2 %all-to-all-start.9 = ((bf16[32,2,1024]{2,1,0:T(2,128)(2,1)}), bf16[32,2,1024]{2,1,0:T(2,128)(2,1)S(1)}, u32[]{:S(2)}, u32[]{:S(2)}) async-start(bf16[32,2,1024]{2,1,0:T(2,128)(2,1)} %reshape.214), calls=%async_computation.9 | async-start | bytes 262144 | tf_op jit(solution)/shard_map/all_to_all | solution.py:57
  278.1 14.1 %all_gather.15 = bf16[512,768]{0,1:T(8,128)(2,1)} all-gather(bf16[512,192]{0,1:T(8,128)(2,1)S(1)} %copy-done.7), channel_id=1, replica_groups=mesh['view'=32,'band'=4,'batch'=4] {'band'}, dimensions={1}, use_global_device_ids=true | all-gather | bytes 983040 | tf_op jit(solution)/shard_map/all_gather | solution.py:83
  292.2 2.3 copy.69
  294.7 2.1 fusion.26
  (72 shorter events, 23.4 us)
Async XLA Ops:
  0.0 7.8 %copy-start = (bf16[768,1536]{1,0:T(8,128)(2,1)S(1)}, bf16[768,1536]{1,0:T(8,128)(2,1)}, u32[]{:S(2)}) copy-start(bf16[768,1536]{1,0:T(8,128)(2,1)} %param.12) | copy-start | bytes 7077892
  2.8 4.6 %copy-start.2 = (bf16[1,8,16,768]{3,2,1,0:T(8,128)(2,1)S(1)}, bf16[1,8,16,768]{3,2,1,0:T(8,128)(2,1)}, u32[]{:S(2)}) copy-start(bf16[1,8,16,768]{3,2,1,0:T(8,128)(2,1)} %param.10) | copy-start | bytes 589828
  2.8 4.8 %copy-start.8 = (f32[768]{0:T(1024)S(1)}, f32[768]{0:T(1024)}, u32[]{:S(2)}) copy-start(f32[768]{0:T(1024)} %param.11) | copy-start | bytes 9220
  2.8 61.7 %all-to-all-start = ((bf16[4,192,1536]{2,1,0:T(8,128)(2,1)}), bf16[4,192,1536]{2,1,0:T(8,128)(2,1)}, u32[]{:S(2)}, u32[]{:S(2)}) async-start(bf16[4,192,1536]{2,1,0:T(8,128)(2,1)} %stack.4), calls=%async_computation | async-start | bytes 4718592 | tf_op jit(solution)/shard_map/all_to_all | solution.py:63
  62.7 0.9 copy-start.3
  62.7 1.2 copy-start.4
  62.8 1.6 copy-start.9
  70.0 70.3 %copy-start.5 = (bf16[192,1536]{1,0:T(8,128)(2,1)S(1)}, bf16[192,1536]{1,0:T(8,128)(2,1)}, u32[]{:S(2)}) copy-start(bf16[192,1536]{1,0:T(8,128)(2,1)} %param.18) | copy-start | bytes 1769476
  141.9 25.4 %all-to-all-start.5 = ((bf16[4,192,1536]{2,1,0:T(8,128)(2,1)}), bf16[4,192,1536]{2,1,0:T(8,128)(2,1)}, u32[]{:S(2)}, u32[]{:S(2)}) async-start(bf16[4,192,1536]{2,1,0:T(8,128)(2,1)} %stack.5), calls=%async_computation.5 | async-start | bytes 4718592 | tf_op jit(solution)/shard_map/all_to_all | solution.py:63
  147.5 0.9 copy-start.6
  167.2 25.8 %all-to-all-start.4 = ((bf16[32,2,1024]{2,1,0:T(2,128)(2,1)}), bf16[32,2,1024]{2,1,0:T(2,128)(2,1)}, u32[]{:S(2)}, u32[]{:S(2)}) async-start(bf16[32,2,1024]{2,1,0:T(2,128)(2,1)} %reshape.212), calls=%async_computation.4 | async-start | bytes 262144 | tf_op jit(solution)/shard_map/all_to_all | solution.py:57
  193.1 2.9 copy-start.10
  248.5 20.0 %all-to-all-start.6 = ((bf16[32,1,16,128]{3,2,1,0:T(8,128)(2,1)}), bf16[32,1,16,128]{3,2,1,0:T(8,128)(2,1)S(1)}, u32[]{:S(2)}, u32[]{:S(2)}) async-start(bf16[32,1,16,128]{3,2,1,0:T(8,128)(2,1)} %bitcast.31), calls=%async_computation.6 | async-start | bytes 262144 | tf_op jit(solution)/shard_map/all_to_all | solution.py:114
  254.9 1.4 copy-start.1
  268.6 9.5 %copy-start.7 = (bf16[512,192]{0,1:T(8,128)(2,1)S(1)}, bf16[512,192]{0,1:T(8,128)(2,1)}, u32[]{:S(2)}) copy-start(bf16[512,192]{0,1:T(8,128)(2,1)} %param.19) | copy-start | bytes 589828
  272.9 21.6 %all-to-all-start.9 = ((bf16[32,2,1024]{2,1,0:T(2,128)(2,1)}), bf16[32,2,1024]{2,1,0:T(2,128)(2,1)S(1)}, u32[]{:S(2)}, u32[]{:S(2)}) async-start(bf16[32,2,1024]{2,1,0:T(2,128)(2,1)} %reshape.214), calls=%async_computation.9 | async-start | bytes 262144 | tf_op jit(solution)/shard_map/all_to_all | solution.py:57
